TPU v7x, 256 devices: a whole 4x4x8 slice. The times are simulated.
256 devices in a mesh: row: 16 (over z_hi, y, core), col: 16 (over z_lo, x).
Axes of the slice: x: 4, y: 4, z: 8 (z_hi: 2, z_lo: 4; z = z_hi * 4 + z_lo), core: 2. Of those that a mesh axis runs over, the one named last changes fastest.
Arguments:
- raster: bfloat16 [64, 512, 2048], P(None, 'row', 'col')
- conv_one: bfloat16 [64, 576], replicated, may hold values from -0.25 to 0.25
- bias_one: float32 [64], replicated, may hold values from -3 to 3
- conv_two: bfloat16 [64, 576], replicated, may hold values from -0.25 to 0.25
- bias_two: float32 [64], replicated, may hold values from -3 to 3
- pos_embed: bfloat16 [64, 16, 64], P(None, 'row', 'col'), may hold values from -6 to 6
- query_embed: bfloat16 [2048, 256], replicated
- w_query: bfloat16 [256, 256], replicated, may hold values from -0.375 to 0.375
- w_key: bfloat16 [64, 256], replicated, may hold values from -0.75 to 0.75
- w_value: bfloat16 [64, 256], replicated, may hold values from -0.75 to 0.75
- w_out: bfloat16 [256, 256], replicated, may hold values from -0.375 to 0.375
- visible: int32 [16, 256], replicated, may hold values from 0 to 1, as said below
Outputs:
- map_queries: bfloat16 [2048, 256], P(('row', 'col'))
Inputs may be any that keep to these rules, and one draw needn't show every extreme that they name: `visible`: every query block sees at least one tile; each block sees a square of tiles around one tile and, independently, about one in eight of the other tiles.
All inputs are finite; a program needn't handle non-finite values.
Results may differ from a plain program's by a relative error of at most 0.035.
Values may be sent and summed in bfloat16 or wider, within the bound.
No kernel may reach another device: no remote copies, remote signals or barrier semaphores. Data moves between devices by JAX's collectives and lax.ppermute only.
A program may use at most 128 MiB of HBM per device.

v0:
```python
import jax
import jax.numpy as jnp
from jax import lax
from jax.sharding import PartitionSpec as P

E = 256
HEADS = 8
HEAD_DIM = 32
PATCH = 32
QBLOCK = 128


def padded_2(shard, sides, width):
    for axis, dim in sides:
        peers, length = (lax.axis_size(axis), shard.shape[dim])
        up = [(i, (i + 1) % peers) for i in range(peers - 1)]
        down = [(j, i) for i, j in up]
        last = lax.slice_in_dim(shard, length - width, length, axis=dim)
        leading = lax.slice_in_dim(shard, 0, width, axis=dim)
        before = lax.ppermute(last, axis, up)
        after = lax.ppermute(leading, axis, down)
        shard = jnp.concatenate([before, shard, after], axis=dim)
    return shard


def merged(part, axis, combine):
    gathered = jax.tree.map(lambda a: lax.all_gather(a, axis), part)

    def take(source):
        return jax.tree.map(lambda a: lax.dynamic_index_in_dim(a, source, 0, False), gathered)

    return lax.fori_loop(
        1, lax.axis_size(axis), lambda source, state: combine(state, take(source)), take(0)
    )


def conv_layer(padded, weight, bias):
    out_rows = padded.shape[1] - 2
    width = padded.shape[2] - 2
    count = min(32, out_rows)
    taps = [padded[:, dy : dy + count, dx : dx + width] for dy in range(3) for dx in range(3)]
    stacked = jnp.concatenate(taps, 0)
    out = jnp.einsum("ok,khw->ohw", weight, stacked, preferred_element_type=jnp.float32)
    pieces = jnp.maximum(out + bias[:, None, None], 0.0)
    return pieces


def combine_partials(first, later):
    peak_a, total_a, mixed_a = first
    peak_b, total_b, mixed_b = later
    top = jnp.maximum(peak_a, peak_b)
    shrink_a = jnp.exp(peak_a - top)
    shrink_b = jnp.exp(peak_b - top)
    count = mixed_a.shape[0]
    mixed = (
        mixed_a.reshape(count, HEADS, HEAD_DIM) * shrink_a[..., None]
        + mixed_b.reshape(count, HEADS, HEAD_DIM) * shrink_b[..., None]
    )
    return (top, total_a * shrink_a + total_b * shrink_b, mixed.reshape(count, E))


def finish(total, mixed, w_out):
    count = mixed.shape[0]
    attended = (
        (mixed.reshape(count, HEADS, HEAD_DIM) / total[..., None])
        .reshape(count, E)
        .astype(jnp.bfloat16)
    )
    return jnp.dot(attended, w_out, preferred_element_type=jnp.float32).astype(jnp.bfloat16)


def on_device(
    raster,
    conv_one,
    bias_one,
    conv_two,
    bias_two,
    pos_embed,
    query_embed,
    w_query,
    w_key,
    w_value,
    w_out,
    visible,
):
    rows = raster.shape[1]
    cols = raster.shape[2]

    def widen(field):
        return padded_2(field, (("row", 1), ("col", 2)), 1)

    first = conv_layer(widen(raster), conv_one, bias_one).astype(jnp.bfloat16)
    second = conv_layer(widen(first), conv_two, bias_two)
    channels = second.shape[0]
    pooled = second.reshape(channels, rows // PATCH, PATCH, cols // PATCH, PATCH).mean(axis=(2, 4))
    tokens = (pooled + pos_embed.astype(jnp.float32)).astype(jnp.bfloat16)
    local_count = rows // PATCH * (cols // PATCH)
    flat = tokens.reshape(channels, local_count).T
    scale = 1.0 / HEAD_DIM**0.5
    all_queries = query_embed.shape[0]
    devices = lax.axis_size("row") * lax.axis_size("col")
    owned = all_queries // devices
    owner = lax.axis_index("row") * lax.axis_size("col") + lax.axis_index("col")
    keys = jnp.dot(flat, w_key, preferred_element_type=jnp.float32).astype(jnp.bfloat16)
    values = jnp.dot(flat, w_value, preferred_element_type=jnp.float32).astype(jnp.bfloat16)
    queries = jnp.dot(query_embed, w_query, preferred_element_type=jnp.float32).astype(jnp.bfloat16)
    tile = lax.axis_index("row") * lax.axis_size("col") + lax.axis_index("col")
    seen_blocks = lax.dynamic_slice_in_dim(visible, tile, 1, 1)[:, 0] > 0
    seen = jnp.repeat(seen_blocks, QBLOCK)
    score = (
        jnp.einsum(
            "qhd,khd->qhk",
            queries.reshape(all_queries, HEADS, HEAD_DIM),
            keys.reshape(local_count, HEADS, HEAD_DIM),
            preferred_element_type=jnp.float32,
        )
        * scale
    )
    top = jnp.max(score, axis=-1)
    weight = jnp.where(seen[:, None, None], jnp.exp(score - top[..., None]), 0.0)
    peak = jnp.where(seen[:, None], top, -1e30)
    total = jnp.sum(weight, axis=-1)
    mixed = jnp.einsum(
        "qhk,khd->qhd",
        weight.astype(jnp.bfloat16),
        values.reshape(local_count, HEADS, HEAD_DIM),
        preferred_element_type=jnp.float32,
    ).reshape(all_queries, E)
    partial_value = merged((peak, total, mixed), "col", combine_partials)
    merged_peak, merged_total, merged_mixed = merged(partial_value, "row", combine_partials)
    own_total = lax.dynamic_slice_in_dim(merged_total, owner * owned, owned, 0)
    own_mixed = lax.dynamic_slice_in_dim(merged_mixed, owner * owned, owned, 0)
    return finish(own_total, own_mixed, w_out)


def solution(mesh):
    in_specs = (
        P(None, "row", "col"),
        P(),
        P(),
        P(),
        P(),
        P(None, "row", "col"),
        P(),
        P(),
        P(),
        P(),
        P(),
        P(),
    )
    out_specs = P(("row", "col"), None)
    return jax.shard_map(
        on_device, mesh=mesh, in_specs=in_specs, out_specs=out_specs, check_vma=False
    )
```

profile of v0, /device:TPU:1, one launch (start us, length us, event | category | flops | bytes accessed | tf_op | source)
XLA Modules:
  0.0 1303.3 jit_solution(8109167960307714745)
XLA Ops:
  7.9 4.6 collective-permute-start
  34.2 3.4 fusion.11
  37.6 3.4 collective-permute-start.4
  65.4 83.3 %all-gather.15.cloned.1.call-done = f32[32768,8]{0,1:T(8,128)} async-done(((f32[2048,8]{0,1:T(8,128)}), f32[32768,8]{0,1:T(8,128)}) %all-gather.15.cloned.1.call-update) | async-done | bytes 1048592 | tf_op jit(solution)/shard_map/all_gather | solution.py:27
  149.6 80.1 %all-gather.11.cloned.1.call-done = f32[16,2048,8]{1,2,0:T(8,128)} async-done(((f32[1,2048,8]{1,2,0:T(8,128)}), f32[16,2048,8]{1,2,0:T(8,128)}) %all-gather.11.cloned.1.call-update) | async-done | bytes 1048592 | tf_op jit(solution)/shard_map/all_gather | solution.py:27
  230.5 365.0 %all-gather.13.cloned.1.call-done = f32[16,2048,256]{2,1,0:T(8,128)} async-done(((f32[1,2048,256]{2,1,0:T(8,128)}), f32[16,2048,256]{2,1,0:T(8,128)}) %all-gather.13.cloned.1.call-update) | async-done | bytes 33554448 | tf_op jit(solution)/shard_map/all_gather | solution.py:27
  599.1 138.8 %while.38 = (s32[]{:T(128)}, f32[2048,8]{0,1:T(8,128)S(1)}, f32[2048,8]{0,1:T(8,128)S(1)}, f32[2048,256]{0,1:T(8,128)}, f32[16,2048,8]{1,2,0:T(8,128)}, /*index=...) while((s32[]{:T(128)}, f32[2048,8]{0,1:T(8,128)S(1)}, ...), condition=%wide.region_5.6_spmd, body=%wide.region_4.5_spmd.sunk | while | flops 1671173 | bytes 15335575 | solution.py:32
  605.0 3.4 fusion.65
  614.2 3.4 fusion.65
  623.5 3.4 fusion.65
  632.7 3.4 fusion.65
  642.0 3.4 fusion.65
  651.2 3.4 fusion.65
  660.5 3.4 fusion.65
  669.7 3.4 fusion.65
  679.0 3.4 fusion.65
  688.2 3.4 fusion.65
  697.5 3.4 fusion.65
  706.7 3.4 fusion.65
  716.0 3.4 fusion.65
  725.2 3.4 fusion.65
  734.5 3.4 fusion.65
  742.1 49.5 %all-gather.17.cloned.1.call-done = f32[32768,8]{0,1:T(8,128)} async-done(((f32[2048,8]{0,1:T(8,128)}), f32[32768,8]{0,1:T(8,128)}) %all-gather.17.cloned.1.call-update) | async-done | bytes 1048592 | tf_op jit(solution)/shard_map/all_gather | solution.py:27
  792.4 53.0 %all-gather.19.cloned.1.call-done = f32[32768,8]{0,1:T(8,128)} async-done(((f32[2048,8]{0,1:T(8,128)}), f32[32768,8]{0,1:T(8,128)}) %all-gather.19.cloned.1.call-update) | async-done | bytes 1048592 | tf_op jit(solution)/shard_map/all_gather | solution.py:27
  846.2 306.0 %all-gather.21.cloned.1.call-done = f32[32768,256]{1,0:T(8,128)} async-done(((f32[2048,256]{1,0:T(8,128)}), f32[32768,256]{1,0:T(8,128)}) %all-gather.21.cloned.1.call-update) | async-done | bytes 33554448 | tf_op jit(solution)/shard_map/all_gather | solution.py:27
  1155.6 138.8 %while.39 = (s32[]{:T(128)}, f32[2048,8]{0,1:T(8,128)S(1)}, f32[2048,8]{0,1:T(8,128)S(1)}, f32[2048,256]{0,1:T(8,128)}, f32[16,2048,8]{1,2,0:T(8,128)}, /*index=...) while((s32[]{:T(128)}, f32[2048,8]{0,1:T(8,128)S(1)}, ...), condition=%wide.region_7.8_spmd, body=%wide.region_6.7_spmd.sunk | while | flops 1671173 | bytes 15335575 | solution.py:32
  1161.6 3.3 fusion.67
  1170.8 3.3 fusion.67
  1180.1 3.3 fusion.67
  1235.6 3.3 fusion.67
  1244.9 3.3 fusion.67
  1254.1 3.3 fusion.67
  (219 shorter events, 270.5 us)
Async XLA Ops:
  6.5 36.4 %copy-start = (bf16[2048,256]{1,0:T(8,128)(2,1)S(1)}, bf16[2048,256]{1,0:T(8,128)(2,1)}, u32[]{:S(2)}) copy-start(bf16[2048,256]{1,0:T(8,128)(2,1)} %param.22) | copy-start | bytes 3145732
  6.5 142.2 %all-gather.15.cloned.1.call-start = ((), (), s32[]{:S(2)}) async-start(), calls=%async_computation.2 | async-start | bytes 1114112 | tf_op jit(solution)/shard_map/all_gather | solution.py:27
  7.9 6.5 collective-permute-start
  12.5 5.1 collective-permute-start.1
  18.1 4.7 collective-permute-start.2
  21.6 4.4 collective-permute-start.3
  26.4 2.3 copy-start.2
  30.9 3.3 copy-start.7
  30.9 3.3 copy-start.13
  34.2 8.7 copy-start.5
  37.6 5.8 copy-start.12
  37.6 6.0 collective-permute-start.4
  41.0 5.1 collective-permute-start.5
  48.5 4.8 collective-permute-start.6
  52.0 4.4 collective-permute-start.7
  58.3 0.9 copy-start.8
  58.3 0.9 copy-start.14
  59.2 1.2 copy-start.9
  59.2 1.2 copy-start.11
  60.3 2.4 copy-start.10
  61.8 167.9 %all-gather.11.cloned.1.call-start = ((), (), s32[]{:S(2)}) async-start(), calls=%async_computation | async-start | bytes 1114112 | tf_op jit(solution)/shard_map/all_gather | solution.py:27
  62.6 532.9 %all-gather.13.cloned.1.call-start = ((), (), s32[]{:S(2)}) async-start(), calls=%async_computation.1 | async-start | bytes 35651584 | tf_op jit(solution)/shard_map/all_gather | solution.py:27
  65.2 726.4 %all-gather.17.cloned.1.call-start = ((), (), s32[]{:S(2)}) async-start(), calls=%async_computation.3 | async-start | bytes 1114112 | tf_op jit(solution)/shard_map/all_gather | solution.py:27
  737.9 0.6 copy-start.4
  737.9 0.7 copy-start.3
  738.5 106.8 %all-gather.19.cloned.1.call-start = ((), (), s32[]{:S(2)}) async-start(), calls=%async_computation.4 | async-start | bytes 1114112 | tf_op jit(solution)/shard_map/all_gather | solution.py:27
  739.1 413.1 %all-gather.21.cloned.1.call-start = ((), (), s32[]{:S(2)}) async-start(), calls=%async_computation.5 | async-start | bytes 35651584 | tf_op jit(solution)/shard_map/all_gather | solution.py:27
  1152.2 1.6 slice-start
  1155.6 140.0 %copy-start.6 = (bf16[256,256]{1,0:T(8,128)(2,1)S(1)}, bf16[256,256]{1,0:T(8,128)(2,1)}, u32[]{:S(2)}) copy-start(bf16[256,256]{1,0:T(8,128)(2,1)} %param.26) | copy-start | bytes 393220
  1294.5 2.0 copy-start.1
Sparse Core Ops, SparseCore 0:
  61.9 86.7 all-gather.14
  150.5 79.1 all-gather.10
  231.5 363.9 all-gather.12
  738.6 52.8 all-gather.16
  794.1 51.1 all-gather.18
  847.9 304.2 all-gather.20
where the time goes:
time: 1310 us; the launch traced here: 1300 us
  waiting for transfers between devices  945 us (72%)
  local copies, waits for them, and re-layouts  175 us (13%)
  other arithmetic  141 us (11%)
  starting transfers between devices  21 us (2%)
  between operations  13.9 us (1%)
    all_gather x6, waiting for transfers between devices, merged(): gathered = jax.tree.map(lambda a: lax.all_gather(a, axis), part)  937 us
    dynamic_slice x65, local copies, waits for them, and re-layouts, take(): lax.dynamic_index_in_dim(a, source, 0, False)  153 us
    add x30, other arithmetic, combine_partials(): mixed_a.reshape(count, HEADS, HEAD_DIM) * shrink_a[..., None]  100 us
    add x30, other arithmetic, combine_partials(): total_a * shrink_a + total_b * shrink_b  28 us
  transfers between devices with their start and end apart: 14, of which 10 were waited for; matrix products, arithmetic and copies ran while one was open for 1% of the time, Pallas kernels for 0%

commit v1 on v0

v1 whole, which is shorter than its diff:
```python
import functools

import jax
import jax.numpy as jnp
from jax import lax
from jax.experimental import pallas as pl
from jax.experimental.pallas import tpu as pltpu
from jax.sharding import PartitionSpec as P

E = 256
HEADS = 8
HEAD_DIM = 32
PATCH = 32
RIM = 2
F32 = jnp.float32
BF16 = jnp.bfloat16


def axis_pos():
    return lax.axis_index("row"), lax.axis_index("col")


def dot(a, b, dims=(((1,), (0,)), ((), ()))):
    return lax.dot_general(a, b, dims, preferred_element_type=F32)


def lanes(shape):
    return lax.broadcasted_iota(jnp.int32, shape, len(shape) - 1)


def sublanes(shape):
    return lax.broadcasted_iota(jnp.int32, shape, len(shape) - 2)


def call(kernel, out_shape, *args, flops=1 << 20, in_specs=None, scratch=()):
    if in_specs is None:
        in_specs = [pl.BlockSpec(memory_space=pltpu.VMEM)] * len(args)
    single = not isinstance(out_shape, (list, tuple))
    outs = [out_shape] if single else list(out_shape)
    result = pl.pallas_call(
        kernel,
        out_shape=outs,
        in_specs=in_specs,
        out_specs=[pl.BlockSpec(memory_space=pltpu.VMEM)] * len(outs),
        scratch_shapes=scratch,
        compiler_params=pltpu.CompilerParams(vmem_limit_bytes=24 << 20),
        cost_estimate=pl.CostEstimate(flops=flops, bytes_accessed=1 << 19, transcendentals=0),
    )(*args)
    return result[0] if single else result


def row_rim_kernel(upper_ref, lower_ref, first_ref, second_ref, up, low):
    r, _ = axis_pos()
    channels, height, width = upper_ref.shape
    up[...] = upper_ref[...].astype(F32).reshape(channels * height, width)
    low[...] = lower_ref[...].astype(F32).reshape(channels * height, width)
    even = lax.rem(r, 2) == 0
    for k in range(RIM):
        top = up[pl.ds(k, channels, stride=height), :]
        bottom = low[pl.ds(height - RIM + k, channels, stride=height), :]
        rows = pl.ds(k * channels, channels)
        first_ref[rows, :] = jnp.where(even, bottom, top).astype(BF16)
        second_ref[rows, :] = jnp.where(even, top, bottom).astype(BF16)


def strip_kernel(raster_ref, left_ref, right_ref, full):
    channels, rows, width = raster_ref.shape
    full[...] = raster_ref[...].astype(F32).reshape(channels * rows, width)
    where = lanes((channels, width))
    left = jnp.zeros((channels, width), F32)
    right = jnp.zeros((channels, width), F32)
    for h in range(rows):
        at = RIM * (h + RIM)
        piece = pltpu.roll(full[pl.ds(h, channels, stride=rows), :], at, 1)
        left = jnp.where((where >= at) & (where < at + RIM), piece, left)
        right = jnp.where((where >= at - RIM) & (where < at), piece, right)
    left_ref[...] = left
    right_ref[...] = pltpu.roll(right, RIM, 1)


def add_corners(strip, above, below, side, rows):
    channels, width = strip.shape
    where = lanes(strip.shape)
    for h, piece in [(k - RIM, above[k]) for k in range(RIM)] + [
        (rows + k, below[k]) for k in range(RIM)
    ]:
        at = RIM * (h + RIM)
        shift = at if side == 0 else (at + RIM) % width
        strip = jnp.where(
            (where >= at) & (where < at + RIM), pltpu.roll(piece, shift, 1), strip
        )
    return strip


def column_rim_kernel(
    rows, left_in, right_in, got_first, got_second, left_ref, right_ref, first_ref, second_ref, above_ref, below_ref
):
    r, c = axis_pos()
    channels = left_in.shape[0]
    even = lax.rem(r, 2) == 0
    above, below = [], []
    for k in range(RIM):
        part = pl.ds(k * channels, channels)
        one, two = got_first[part, :].astype(F32), got_second[part, :].astype(F32)
        above.append(jnp.where(even, two, one))
        below.append(jnp.where(even, one, two))
        above_ref[k] = above[k]
        below_ref[k] = below[k]
    left = add_corners(left_in[...], above, below, 0, rows)
    right = add_corners(right_in[...], above, below, 1, rows)
    left_ref[...] = left
    right_ref[...] = right
    even = lax.rem(c, 2) == 0
    first_ref[...] = jnp.where(even, right, left).astype(BF16)
    second_ref[...] = jnp.where(even, left, right).astype(BF16)


def conv_kernel(
    grid, raster_ref, above_ref, below_ref, own_left_ref, own_right_ref, got_first, got_second,
    one_ref, bias_one_ref, two_ref, bias_two_ref, pos_ref, out_ref, full, taps_one, taps_two,
):
    r, c = axis_pos()
    n_rows, n_cols = grid
    channels, rows, width = raster_ref.shape
    full[...] = raster_ref[...].astype(F32).reshape(channels * rows, width)
    shape = (channels, width)
    where = lanes(shape)
    even = lax.rem(c, 2) == 0
    one, two = got_first[...].astype(F32), got_second[...].astype(F32)
    far_left = jnp.where(even, two, one)
    far_right = jnp.where(even, one, two)

    def store_taps(taps, i, field, fill_left, fill_right):
        before = jnp.where(where == 0, fill_left, pltpu.roll(field, 1, 1))
        after = jnp.where(where == width - 1, fill_right, pltpu.roll(field, width - 1, 1))
        taps[i, 0:channels, :] = before.astype(BF16)
        taps[i, channels : 2 * channels, :] = field.astype(BF16)
        taps[i, 2 * channels : 3 * channels, :] = after.astype(BF16)

    def turn(x, shift):
        return pltpu.roll(x, shift % width, 1)

    for i in range(rows + 2 * RIM):
        h = i - RIM
        if h < 0:
            field = above_ref[i]
        elif h >= rows:
            field = below_ref[h - rows]
        else:
            field = full[pl.ds(h, channels, stride=rows), :]
        store_taps(
            taps_one, i, field,
            turn(far_left, -(RIM * i + RIM - 1)), turn(far_right, width - 1 - RIM * i),
        )

    weight_one, weight_two = one_ref[...], two_ref[...]
    bias_one = bias_one_ref[...]
    bias_two = bias_two_ref[...]

    own_left, own_right = own_left_ref[...], own_right_ref[...]
    left_taps = [far_left, turn(far_left, -1), own_left]
    right_taps = [turn(own_right, -1), far_right, turn(far_right, -1)]
    edge = jnp.concatenate(
        [
            jnp.concatenate([turn(a, -RIM * dy), turn(b, -RIM * dy)], axis=1).astype(BF16)
            for dy in (-1, 0, 1)
            for a, b in zip(left_taps, right_taps)
        ],
        axis=0,
    )
    edge_first = jnp.maximum(dot(weight_one, edge) + bias_one, 0.0)
    edge_left = jnp.where(c > 0, edge_first[:, :width], 0.0)
    edge_right = jnp.where(c < n_cols - 1, edge_first[:, width:], 0.0)

    def pair(taps, i):
        a = taps[i : i + 3].reshape(9 * channels, width)
        b = taps[i + 1 : i + 4].reshape(9 * channels, width)
        return jnp.concatenate([a, b], axis=1)

    for i in range(0, rows + 2, 2):
        both = jnp.maximum(dot(weight_one, pair(taps_one, i)) + bias_one, 0.0)
        for k in range(2):
            field = both[:, k * width : (k + 1) * width]
            at = RIM * (i + k + 1)
            fill_left, fill_right = turn(edge_left, -at), turn(edge_right, width - 1 - at)
            if i + k == 0 or i + k == rows + 1:
                keep = (r > 0) if i + k == 0 else (r < n_rows - 1)
                field = jnp.where(keep, field, 0.0)
                fill_left = jnp.where(keep, fill_left, 0.0)
                fill_right = jnp.where(keep, fill_right, 0.0)
            store_taps(taps_two, i + k, field, fill_left, fill_right)

    total = jnp.zeros((channels, 2 * width), F32)
    for i in range(0, rows, 2):
        total = total + jnp.maximum(dot(weight_two, pair(taps_two, i)) + bias_two, 0.0)
    total = total[:, :width] + total[:, width:]
    patches = width // PATCH
    member = (sublanes((8, width)) == lanes((8, width)) // PATCH).astype(F32)
    pooled = lax.dot_general(
        member, total, (((1,), (1,)), ((), ())),
        precision=lax.Precision.HIGHEST, preferred_element_type=F32,
    )
    tokens = pooled[:patches] * (1.0 / (PATCH * PATCH)) + pos_ref[...]
    flat = jnp.concatenate([tokens[k : k + 1] for k in range(patches)], axis=1)
    block = jnp.concatenate([flat[:, :128], flat[:, 128:]], axis=0).astype(BF16)
    out_ref[...] = jnp.broadcast_to(block[None], out_ref.shape)


def query_kernel(n_blocks, patches, embed_ref, w_query_ref, w_key_ref, visible_ref, out_ref, seen_ref):
    r, c = axis_pos()
    del c
    owned = embed_ref.shape[0]
    channels = w_key_ref.shape[0]
    queries = dot(embed_ref[...], w_query_ref[...]).astype(BF16).astype(F32)
    wide = jnp.concatenate([queries] * (patches * HEADS), axis=0)
    head = lax.rem(sublanes(wide.shape) // owned, HEADS)
    wide = jnp.where(head == lanes(wide.shape) // HEAD_DIM, wide, 0.0).astype(BF16)
    keys = jnp.concatenate([w_key_ref[...]] * patches, axis=0)
    folded = dot(wide, keys, (((1,), (1,)), ((), ()))) * (1.0 / HEAD_DIM**0.5)
    same = sublanes(folded.shape) // (HEADS * owned) == lanes(folded.shape) // channels
    out_ref[...] = jnp.where(same, folded, 0.0).astype(BF16)
    seen_ref[...] = visible_ref[pl.ds(r, 1), :]


def attend_kernel(folded_ref, seen_ref, tokens_ref, w_value_ref, w_out_ref, out_ref):
    owned = out_ref.shape[0]
    channels = w_value_ref.shape[0]
    tokens = tokens_ref[...]
    patches = tokens.shape[1] // channels
    group = HEADS * owned
    score = dot(folded_ref[...], tokens, (((1,), (1,)), ((), ())))
    seen = seen_ref[...] > 0
    score = jnp.where(seen, score, -1e30)
    parts = [score[p * group : (p + 1) * group] for p in range(patches)]
    peak = jnp.max(functools.reduce(jnp.maximum, parts), axis=1, keepdims=True)
    weights = [jnp.where(seen, jnp.exp(p - peak), 0.0) for p in parts]
    total = jnp.sum(functools.reduce(jnp.add, weights), axis=1, keepdims=True)
    stacked = jnp.concatenate(weights, axis=0).astype(BF16)
    mixed = dot(stacked, tokens)
    same = sublanes(mixed.shape) // group == lanes(mixed.shape) // channels
    mixed = jnp.where(same, mixed, 0.0)
    inverse = 1.0 / total
    mixed = (mixed * jnp.concatenate([inverse] * patches, axis=0)).astype(BF16)
    values = jnp.concatenate([w_value_ref[...]] * patches, axis=0)
    heads = dot(mixed, values)
    head = lax.rem(sublanes(heads.shape) // owned, HEADS)
    heads = jnp.where(head == lanes(heads.shape) // HEAD_DIM, heads, 0.0)
    attended = functools.reduce(
        jnp.add, [heads[k * owned : (k + 1) * owned] for k in range(patches * HEADS)]
    )
    out_ref[...] = dot(attended.astype(BF16), w_out_ref[...]).astype(BF16)


def swaps(n, start):
    pairs = [(i, i + 1) for i in range(start, n - 1, 2)]
    return pairs + [(j, i) for i, j in pairs]


def on_device(
    raster, conv_one, bias_one, conv_two, bias_two, pos_embed,
    query_embed, w_query, w_key, w_value, w_out, visible,
):
    channels, rows, width = raster.shape
    n_rows, n_cols = lax.axis_size("row"), lax.axis_size("col")
    devices = n_rows * n_cols
    patches = width // PATCH
    owned = query_embed.shape[0] // devices
    owner = lax.axis_index("row") * n_cols + lax.axis_index("col")
    tile = jax.ShapeDtypeStruct((channels, width), F32)
    half = jax.ShapeDtypeStruct((channels, width), BF16)
    rim = jax.ShapeDtypeStruct((RIM * channels, width), BF16)

    whole = pl.BlockSpec(memory_space=pltpu.VMEM)
    last = rows // 8 - 1
    first_rows, second_rows = pl.pallas_call(
        row_rim_kernel,
        grid=(1,),
        out_shape=[rim, rim],
        in_specs=[
            pl.BlockSpec((channels, 8, width), lambda i: (0, 0, 0)),
            pl.BlockSpec((channels, 8, width), lambda i: (0, last, 0)),
        ],
        out_specs=[whole, whole],
        scratch_shapes=[pltpu.VMEM((channels * 8, width), F32)] * 2,
        compiler_params=pltpu.CompilerParams(vmem_limit_bytes=24 << 20),
        cost_estimate=pl.CostEstimate(flops=1 << 20, bytes_accessed=1 << 18, transcendentals=0),
    )(raster, raster)
    got_first = lax.ppermute(first_rows, "row", swaps(n_rows, 0))
    got_second = lax.ppermute(second_rows, "row", swaps(n_rows, 1))
    left, right = call(
        strip_kernel, [tile, tile], raster, scratch=[pltpu.VMEM((channels * rows, width), F32)]
    )
    pair = jax.ShapeDtypeStruct((RIM, channels, width), F32)
    left, right, first_cols, second_cols, above, below = call(
        functools.partial(column_rim_kernel, rows),
        [tile, tile, half, half, pair, pair],
        left, right, got_first, got_second,
    )
    got_first = lax.ppermute(first_cols, "col", swaps(n_cols, 0))
    got_second = lax.ppermute(second_cols, "col", swaps(n_cols, 1))

    own_embed = lax.dynamic_slice_in_dim(query_embed, owner * owned, owned, 0)
    size = patches * HEADS * owned
    folded, seen = call(
        functools.partial(query_kernel, n_rows, patches),
        [
            jax.ShapeDtypeStruct((size, patches * channels), BF16),
            jax.ShapeDtypeStruct((1, devices), jnp.int32),
        ],
        own_embed, w_query, w_key, visible,
    )

    position = pos_embed.astype(F32).reshape(channels, patches).T
    block = call(
        functools.partial(conv_kernel, (n_rows, n_cols)),
        jax.ShapeDtypeStruct((devices, patches * channels // 128, 128), BF16),
        raster, above, below, left, right, got_first, got_second,
        conv_one, bias_one.reshape(channels, 1), conv_two, bias_two.reshape(channels, 1), position,
        flops=1 << 30,
        scratch=[
            pltpu.VMEM((channels * rows, width), F32),
            pltpu.VMEM((rows + 2 * RIM, 3 * channels, width), BF16),
            pltpu.VMEM((rows + 2, 3 * channels, width), BF16),
        ],
    )
    everyone = lax.all_to_all(block, ("row", "col"), 0, 0, tiled=True)
    tokens = everyone.reshape(devices, patches * channels)
    return call(
        attend_kernel,
        jax.ShapeDtypeStruct((owned, E), BF16),
        folded, seen, tokens, w_value, w_out,
    )


def solution(mesh):
    in_specs = (
        P(None, "row", "col"),
        P(),
        P(),
        P(),
        P(),
        P(None, "row", "col"),
        P(),
        P(),
        P(),
        P(),
        P(),
        P(),
    )
    out_specs = P(("row", "col"), None)
    return jax.shard_map(
        on_device, mesh=mesh, in_specs=in_specs, out_specs=out_specs, check_vma=False
    )
```

time: 1310 us -> 53.4 us (0.04)
  waiting for transfers between devices: 945 us -> 15.3 us
  local copies, waits for them, and re-layouts: 175 us -> 3.59 us
  other arithmetic: 141 us -> 0.01 us
  between operations: 13.9 us -> 0.17 us
    all_gather x6 -> x0, waiting for transfers between devices: 937 us -> none  [merged(): gathered = jax.tree.map(lambda a: lax.all_gather(a, axis), part)]
    dynamic_slice x66 -> x1, local copies, waits for them, and re-layouts: 153 us -> 0.01 us  [on_device(): own_embed = lax.dynamic_slice_in_dim(query_embed, owner * owned, owned, 0)]
    add x60 -> x0, other arithmetic: 128 us -> none  [the longest x30 100 us: combine_partials(): mixed_a.reshape(count, HEADS, HEAD_DIM) * shrink_a[..., None]]
    all_to_all x0 -> x1, starting transfers between devices: none -> 21.5 us  [on_device(): everyone = lax.all_to_all(block, ('row', 'col'), 0, 0, tiled=True)]
    ppermute x8 -> x4, starting transfers between devices: 20.6 us -> 5.95 us  [the longest x1 3.29 us: on_device(): got_first = lax.ppermute(first_rows, 'row', swaps(n_rows, 0))]
  transfers between devices with their start and end apart: 14 -> 5, of which waited for: 10 -> 3; matrix products, arithmetic and copies ran while one was open for 1% -> 0% of each run, Pallas kernels for 0% -> 2%
where the time goes in v1:
time: 53.4 us; the launch traced here: 53.1 us
  starting transfers between devices  27.4 us (51%)
  waiting for transfers between devices  15.3 us (29%)
  Pallas kernels  6.56 us (12%)
  local copies, waits for them, and re-layouts  3.59 us (7%)
    all_to_all x1, starting transfers between devices, on_device(): everyone = lax.all_to_all(block, ('row', 'col'), 0, 0, tiled=True)  21.5 us
    all_to_all x1, waiting for transfers between devices, on_device(): everyone = lax.all_to_all(block, ('row', 'col'), 0, 0, tiled=True)  11.8 us
    pallas_call x5, Pallas kernels, call(): pl.pallas_call(kernel, out_shape=outs, in_specs=in_specs, out_specs=[pl.B...  6.46 us
    unnamed x27, local copies, waits for them, and re-layouts  3.39 us
    ppermute x1, starting transfers between devices, on_device(): got_first = lax.ppermute(first_rows, 'row', swaps(n_rows, 0))  3.29 us
    ppermute x1, waiting for transfers between devices, on_device(): got_second = lax.ppermute(second_rows, 'row', swaps(n_rows, 1))  2.49 us
    ppermute x1, starting transfers between devices, on_device(): got_second = lax.ppermute(second_rows, 'row', swaps(n_rows, 1))  1.91 us
  transfers between devices with their start and end apart: 5, of which 3 were waited for; matrix products, arithmetic and copies ran while one was open for 0% of the time, Pallas kernels for 2%

profile of v1, /device:TPU:1, one launch (start us, length us, event | category | flops | bytes accessed | tf_op | source)
XLA Modules:
  0.0 53.1 jit_solution(11503652830033699533)
XLA Ops:
  0.0 0.0 copy-start
  0.0 1.1 %copy-done.1 = bf16[64,32,128]{2,1,0:T(8,128)(2,1)S(1)} copy-done((bf16[64,32,128]{2,1,0:T(8,128)(2,1)S(1)}, bf16[64,32,128]{2,1,0:T(8,128)(2,1)}, u32[]{:S(2)}) %copy-start.1) | copy-done | bytes 524312
  1.1 0.1 shard_map.120
  1.2 0.0 copy-start.2
  1.2 3.3 %collective-permute-start = (bf16[128,128]{1,0:T(8,128)(2,1)S(1)}, bf16[128,128]{1,0:T(8,128)(2,1)S(1)}, u32[]{:S(2)}, u32[]{:S(2)}) collective-permute-start(bf16[128,128]{1,0:T(8,128)(2,1)S(1)} %get-tuple-element.21), channel_id=1, source_target_pairs={{0,16},{32,48},{64,80},{96,112},{128,144},{160,176},{192,208},{224... | collective-permute-start | bytes 98312 | tf_op jit(solution)/shard_map/ppermute | solution.py:288
  4.5 1.9 %collective-permute-start.1 = (bf16[128,128]{1,0:T(8,128)(2,1)S(1)}, bf16[128,128]{1,0:T(8,128)(2,1)S(1)}, u32[]{:S(2)}, u32[]{:S(2)}) collective-permute-start(bf16[128,128]{1,0:T(8,128)(2,1)S(1)} %get-tuple-element.22), channel_id=1, source_target_pairs={{16,32},{48,64},{80,96},{112,128},{144,160},{176,192},{208,224},{3... | collective-permute-start | bytes 98312 | tf_op jit(solution)/shard_map/ppermute | solution.py:289
  6.5 0.0 copy-start.10
  6.5 0.0 copy-start.11
  6.5 1.0 %shard_map.119 = (f32[64,128]{1,0:T(8,128)S(1)}, f32[64,128]{1,0:T(8,128)S(1)}) custom-call(bf16[64,32,128]{2,1,0:T(8,128)(2,1)S(1)} %copy-done.1), custom_call_target="tpu_custom_call" | custom-call | flops 1048576 | bytes 524288 | tf_op jit(solution)/shard_map/pallas_call | solution.py:40
  7.5 0.0 collective-permute-done.got_first
  7.5 2.5 %collective-permute-done.1.got_second = bf16[128,128]{1,0:T(8,128)(2,1)S(1)} collective-permute-done((bf16[128,128]{1,0:T(8,128)(2,1)S(1)}, bf16[128,128]{1,0:T(8,128)(2,1)S(1)}, u32[]{:S(2)}, u32[]{:S(2)}) %collective-permute-start.1) | collective-permute-done | bytes 32800 | tf_op jit(solution)/shard_map/ppermute | solution.py:289
  9.9 0.1 shard_map.121
  10.1 0.1 collective-permute-start.2
  10.2 0.7 %collective-permute-start.3 = (bf16[64,128]{1,0:T(8,128)(2,1)S(1)}, bf16[64,128]{1,0:T(8,128)(2,1)S(1)}, u32[]{:S(2)}, u32[]{:S(2)}) collective-permute-start(bf16[64,128]{1,0:T(8,128)(2,1)S(1)} %get-tuple-element.28), channel_id=1, source_target_pairs={{1,2},{3,4},{5,6},{7,8},{9,10},{11,12},{13,14},{2,1},{4,3},{6,5},{... | collective-permute-start | bytes 49160 | tf_op jit(solution)/shard_map/ppermute | solution.py:300
  10.8 0.0 copy-done.10
  10.9 0.0 copy-done.11
  10.9 0.1 copy.13.bias_one_ref
  11.0 0.7 %copy-done.12 = f32[64]{0:T(128)S(1)} copy-done((f32[64]{0:T(128)S(1)}, f32[64]{0:T(128)}, u32[]{:S(2)}) %copy-start.12) | copy-done | bytes 280
  11.6 0.1 copy.14.bias_two_ref
  11.7 1.0 %collective-permute-done.2.got_first = bf16[64,128]{1,0:T(8,128)(2,1)S(1)} collective-permute-done((bf16[64,128]{1,0:T(8,128)(2,1)S(1)}, bf16[64,128]{1,0:T(8,128)(2,1)S(1)}, u32[]{:S(2)}, u32[]{:S(2)}) %collective-permute-start.2) | collective-permute-done | bytes 16416 | tf_op jit(solution)/shard_map/ppermute | solution.py:299
  12.7 0.0 collective-permute-done.3.got_second
  12.7 0.0 copy-done.2
  12.8 3.7 %shard_map.122 = bf16[256,2,128]{2,1,0:T(2,128)(2,1)} custom-call(bf16[64,32,128]{2,1,0:T(8,128)(2,1)S(1)} %copy-done.2, f32[2,64,128]{2,1,0:T(8,128)S(1)} %get-tuple-element.23.above_ref, f32[2,64,128]{2,1,0:T(8,128)S(1)} %get-tuple-element.24.below_ref, f32[64,128]{1,0:T(8,128)S(1)} %get-tuple-element.25.own_left_ref, ...), custom_call_target="tpu_custom_call" | custom-call | flops 1073741824 | bytes 524288 | tf_op jit(solution)/shard_map/pallas_call | solution.py:40
  16.4 21.5 %all-to-all-start = ((bf16[256,2,128]{2,1,0:T(2,128)(2,1)}), bf16[256,2,128]{2,1,0:T(2,128)(2,1)S(1)}, u32[]{:S(2)}, u32[]{:S(2)}) async-start(bf16[256,2,128]{2,1,0:T(2,128)(2,1)} %shard_map.122), calls=%async_computation | async-start | bytes 262144 | tf_op jit(solution)/shard_map/all_to_all | solution.py:326
  37.9 0.0 copy-start.7
  38.0 0.0 copy-done
  38.0 0.7 %copy-done.7 = s32[16,256]{1,0:T(8,128)S(1)} copy-done((s32[16,256]{1,0:T(8,128)S(1)}, s32[16,256]{1,0:T(8,128)}, u32[]{:S(2)}) %copy-start.7) | copy-done | bytes 16408
  38.7 0.3 shard_map.118
  39.0 11.8 %all-to-all-done = bf16[256,2,128]{2,1,0:T(2,128)(2,1)S(1)} async-done(((bf16[256,2,128]{2,1,0:T(2,128)(2,1)}), bf16[256,2,128]{2,1,0:T(2,128)(2,1)S(1)}, u32[]{:S(2)}, u32[]{:S(2)}) %all-to-all-start) | async-done | bytes 131104 | tf_op jit(solution)/shard_map/all_to_all | solution.py:326
  50.8 0.9 %copy-done.4 = bf16[256,256]{1,0:T(8,128)(2,1)S(1)} copy-done((bf16[256,256]{1,0:T(8,128)(2,1)S(1)}, bf16[256,256]{1,0:T(8,128)(2,1)}, u32[]{:S(2)}) %copy-start.4) | copy-done | bytes 131096
  51.7 0.0 copy-done.6
  51.7 1.4 %shard_map.123 = bf16[8,256]{1,0:T(8,128)(2,1)} custom-call(bf16[256,256]{1,0:T(8,128)(2,1)S(1)} %get-tuple-element.17.folded_ref, s32[1,256]{1,0:T(1,128)S(1)} %get-tuple-element.18.seen_ref, bf16[256,256]{1,0:T(8,128)(2,1)S(1)} %bitcast.11, bf16[64,256]{1,0:T(8,128)(2,1)S(1)} %copy-done.6, bf16[256,256]{1,0:T(8,128)(2,1)S(1)} %copy-done.4), custom_call_target="tpu_custom_call" | custom-call | flops 1048576 | bytes 524288 | tf_op jit(solution)/shard_map/pallas_call | solution.py:40
  (15 shorter events, 0.1 us)
Async XLA Ops:
  0.0 38.0 %copy-start = (bf16[2048,256]{1,0:T(8,128)(2,1)S(1)}, bf16[2048,256]{1,0:T(8,128)(2,1)}, u32[]{:S(2)}) copy-start(bf16[2048,256]{1,0:T(8,128)(2,1)} %param.18) | copy-start | bytes 3145732
  0.0 1.1 %copy-start.1 = (bf16[64,32,128]{2,1,0:T(8,128)(2,1)S(1)}, bf16[64,32,128]{2,1,0:T(8,128)(2,1)}, u32[]{:S(2)}) copy-start(bf16[64,32,128]{2,1,0:T(8,128)(2,1)} %raster_ref.3) | copy-start | bytes 1572868
  1.2 11.5 %copy-start.2 = (bf16[64,32,128]{2,1,0:T(8,128)(2,1)S(1)}, bf16[64,32,128]{2,1,0:T(8,128)(2,1)}, u32[]{:S(2)}) copy-start(bf16[64,32,128]{2,1,0:T(8,128)(2,1)} %raster_ref.3) | copy-start | bytes 1572868
  1.2 6.2 %collective-permute-start = (bf16[128,128]{1,0:T(8,128)(2,1)S(1)}, bf16[128,128]{1,0:T(8,128)(2,1)S(1)}, u32[]{:S(2)}, u32[]{:S(2)}) collective-permute-start(bf16[128,128]{1,0:T(8,128)(2,1)S(1)} %get-tuple-element.21), channel_id=1, source_target_pairs={{0,16},{32,48},{64,80},{96,112},{128,144},{160,176},{192,208},{224... | collective-permute-start | bytes 98312 | tf_op jit(solution)/shard_map/ppermute | solution.py:288
  4.5 5.4 %collective-permute-start.1 = (bf16[128,128]{1,0:T(8,128)(2,1)S(1)}, bf16[128,128]{1,0:T(8,128)(2,1)S(1)}, u32[]{:S(2)}, u32[]{:S(2)}) collective-permute-start(bf16[128,128]{1,0:T(8,128)(2,1)S(1)} %get-tuple-element.22), channel_id=1, source_target_pairs={{16,32},{48,64},{80,96},{112,128},{144,160},{176,192},{208,224},{3... | collective-permute-start | bytes 98312 | tf_op jit(solution)/shard_map/ppermute | solution.py:289
  6.5 4.4 %copy-start.10 = (bf16[64,1,4]{0,2,1:T(4,128)(2,1)S(1)}, bf16[64,1,4]{0,2,1:T(4,128)(2,1)}, u32[]{:S(2)}) copy-start(bf16[64,1,4]{0,2,1:T(4,128)(2,1)} %param.17) | copy-start | bytes 1540
  6.5 4.4 %copy-start.11 = (f32[64]{0:T(128)S(1)}, f32[64]{0:T(128)}, u32[]{:S(2)}) copy-start(f32[64]{0:T(128)} %param.14) | copy-start | bytes 772
  9.9 2.8 %copy-start.8 = (bf16[64,576]{1,0:T(8,128)(2,1)S(1)}, bf16[64,576]{1,0:T(8,128)(2,1)}, u32[]{:S(2)}) copy-start(bf16[64,576]{1,0:T(8,128)(2,1)} %one_ref.1) | copy-start | bytes 221188
  9.9 2.8 %copy-start.9 = (bf16[64,576]{1,0:T(8,128)(2,1)S(1)}, bf16[64,576]{1,0:T(8,128)(2,1)}, u32[]{:S(2)}) copy-start(bf16[64,576]{1,0:T(8,128)(2,1)} %two_ref.1) | copy-start | bytes 221188
  10.1 2.7 %collective-permute-start.2 = (bf16[64,128]{1,0:T(8,128)(2,1)S(1)}, bf16[64,128]{1,0:T(8,128)(2,1)S(1)}, u32[]{:S(2)}, u32[]{:S(2)}) collective-permute-start(bf16[64,128]{1,0:T(8,128)(2,1)S(1)} %get-tuple-element.27), channel_id=1, source_target_pairs={{0,1},{2,3},{4,5},{6,7},{8,9},{10,11},{12,13},{14,15},{1,0},{3,2},... | collective-permute-start | bytes 49160 | tf_op jit(solution)/shard_map/ppermute | solution.py:299
  10.2 2.6 %collective-permute-start.3 = (bf16[64,128]{1,0:T(8,128)(2,1)S(1)}, bf16[64,128]{1,0:T(8,128)(2,1)S(1)}, u32[]{:S(2)}, u32[]{:S(2)}) collective-permute-start(bf16[64,128]{1,0:T(8,128)(2,1)S(1)} %get-tuple-element.28), channel_id=1, source_target_pairs={{1,2},{3,4},{5,6},{7,8},{9,10},{11,12},{13,14},{2,1},{4,3},{6,5},{... | collective-permute-start | bytes 49160 | tf_op jit(solution)/shard_map/ppermute | solution.py:300
  11.0 0.7 %copy-start.12 = (f32[64]{0:T(128)S(1)}, f32[64]{0:T(128)}, u32[]{:S(2)}) copy-start(f32[64]{0:T(128)} %param.16) | copy-start | bytes 772
  16.4 21.6 %copy-start.3 = (bf16[256,256]{1,0:T(8,128)(2,1)S(1)}, bf16[256,256]{1,0:T(8,128)(2,1)}, u32[]{:S(2)}) copy-start(bf16[256,256]{1,0:T(8,128)(2,1)} %w_query_ref.1) | copy-start | bytes 393220
  16.4 21.6 %copy-start.5 = (bf16[64,256]{1,0:T(8,128)(2,1)S(1)}, bf16[64,256]{1,0:T(8,128)(2,1)}, u32[]{:S(2)}) copy-start(bf16[64,256]{1,0:T(8,128)(2,1)} %w_key_ref.1) | copy-start | bytes 98308
  16.4 34.4 %all-to-all-start = ((bf16[256,2,128]{2,1,0:T(2,128)(2,1)}), bf16[256,2,128]{2,1,0:T(2,128)(2,1)S(1)}, u32[]{:S(2)}, u32[]{:S(2)}) async-start(bf16[256,2,128]{2,1,0:T(2,128)(2,1)} %shard_map.122), calls=%async_computation | async-start | bytes 262144 | tf_op jit(solution)/shard_map/all_to_all | solution.py:326
  37.9 0.7 %copy-start.7 = (s32[16,256]{1,0:T(8,128)S(1)}, s32[16,256]{1,0:T(8,128)}, u32[]{:S(2)}) copy-start(s32[16,256]{1,0:T(8,128)} %visible_ref.1) | copy-start | bytes 49156
  50.8 0.9 %copy-start.4 = (bf16[256,256]{1,0:T(8,128)(2,1)S(1)}, bf16[256,256]{1,0:T(8,128)(2,1)}, u32[]{:S(2)}) copy-start(bf16[256,256]{1,0:T(8,128)(2,1)} %w_out_ref.1) | copy-start | bytes 393220
  50.8 0.9 %copy-start.6 = (bf16[64,256]{1,0:T(8,128)(2,1)S(1)}, bf16[64,256]{1,0:T(8,128)(2,1)}, u32[]{:S(2)}) copy-start(bf16[64,256]{1,0:T(8,128)(2,1)} %w_value_ref.1) | copy-start | bytes 98308
